TPU v7x, 32 devices: a whole 2x2x4 slice. The times are simulated.
32 devices in a mesh: space: 16 (over z, y, core), grp: 2 (over x).
Axes of the slice: x: 2, y: 2, z: 4, core: 2. Of those that a mesh axis runs over, the one named last changes fastest.
Arguments:
- diag_blocks: float32 [16, 2, 128, 128], P('space', 'grp'), may hold values from -0.4 to 0.4
- x_coupling: float32 [16, 2, 128, 128], P('space', 'grp'), may hold values from -0.35 to 0.35
- y_coupling: float32 [16, 2, 128, 128], P('space', 'grp'), may hold values from -0.35 to 0.35
- levels: float32 [16, 2, 128], P('space', 'grp'), may hold values from -2 to 2
- listed: int32 [16, 2, 2], P('space', 'grp'), may hold values 0 or 1
Outputs:
- density_diag: float32 [16, 2, 128, 128], P('space', 'grp')
- density_x: float32 [16, 2, 128, 128], P('space', 'grp')
- density_y: float32 [16, 2, 128, 128], P('space', 'grp')
Inputs may be any that keep to these rules, and one draw needn't show every extreme that they name: listed[i,j,0] keeps the coupling of block (i,j) with (i+1,j), listed[i,j,1] that with (i,j+1).
All inputs are finite; a program needn't handle non-finite values.
Results may differ from a plain program's by a relative error of at most 0.0037.
Values sent between devices are 32-bit elements; how exact they have to be, the bound alone decides.
A program may use at most 64 MiB of HBM per device.

v0:
```python
import jax
import jax.numpy as jnp
from jax import lax
from jax.sharding import PartitionSpec as P

hubbard = 1.0


def shifted(x, axis, by):
    peers = lax.axis_size(axis)
    pairs = [(i, i + by) for i in range(peers) if 0 <= i + by < peers]
    return lax.ppermute(x, axis, pairs)


def symmetric(matrix):
    return 0.5 * (matrix + matrix.T)


def assemble(center, nbr_diag, nbr_coup):
    block_width = center.shape[0]
    zero_block = jnp.zeros((block_width, block_width), center.dtype)
    top_row = jnp.concatenate([center] + [nbr_coup[member].T for member in range(4)], axis=1)
    row_list = [top_row]
    for member in range(4):
        pieces = [nbr_coup[member]] + [
            nbr_diag[member] if column_slot == member else zero_block for column_slot in range(4)
        ]
        row_list.append(jnp.concatenate(pieces, axis=1))
    return jnp.concatenate(row_list, axis=0)


def density_column(matrix):
    order_size = matrix.shape[0]
    block_width = order_size // 5
    matrix_half = matrix.astype(jnp.bfloat16)
    square = jnp.dot(matrix_half, matrix_half, preferred_element_type=jnp.float32)
    square_half = square.astype(jnp.bfloat16)
    fourth = jnp.dot(square_half, square_half, preferred_element_type=jnp.float32)
    scale_four = jnp.sqrt(jnp.sum(fourth * fourth) + 1e-06)
    scale_two = jnp.sqrt(scale_four)
    scale_one = jnp.sqrt(scale_two)
    identity = jnp.eye(order_size, dtype=jnp.float32)
    initial = (matrix / scale_one).astype(jnp.bfloat16)
    factor = (3.0 * identity - square / scale_two).astype(jnp.bfloat16)
    iterate = (0.5 * jnp.dot(initial, factor, preferred_element_type=jnp.float32)).astype(
        jnp.bfloat16
    )
    column = iterate[:, :block_width]
    applied_once = jnp.dot(iterate, column, preferred_element_type=jnp.float32).astype(jnp.bfloat16)
    applied_twice = jnp.dot(iterate, applied_once, preferred_element_type=jnp.float32)
    sign_part = 0.5 * (3.0 * column.astype(jnp.float32) - applied_twice)
    density = 0.5 * (identity[:, :block_width] - sign_part)
    return density.reshape(5, block_width, block_width)


def neighbour_blocks(own_diag, own_x, own_y):
    from_low_x = shifted(jnp.stack([own_diag, own_x]), "space", 1)
    from_high_x = shifted(own_diag, "space", -1)
    from_low_y = shifted(jnp.stack([own_diag, own_y]), "grp", 1)
    from_high_y = shifted(own_diag, "grp", -1)
    nbr_diag = jnp.stack([from_low_x[0], from_high_x, from_low_y[0], from_high_y])
    nbr_coup = jnp.stack([from_low_x[1], own_x.T, from_low_y[1], own_y.T])
    return (nbr_diag, nbr_coup)


def averaged(columns):
    below_x = shifted(columns[1], "space", -1)
    below_y = shifted(columns[3], "grp", -1)
    return (symmetric(columns[0]), 0.5 * (columns[2].T + below_x), 0.5 * (columns[4].T + below_y))


def per_device(diag_blocks, x_coupling, y_coupling, levels, listed):
    block_width = diag_blocks.shape[-1]
    identity = jnp.eye(block_width, dtype=jnp.float32)
    index_x = lax.axis_index("space")
    index_y = lax.axis_index("grp")
    count_x = lax.axis_size("space")
    count_y = lax.axis_size("grp")
    flag_x = listed[0, 0, 0].astype(jnp.float32) * (index_x < count_x - 1).astype(jnp.float32)
    flag_y = listed[0, 0, 1].astype(jnp.float32) * (index_y < count_y - 1).astype(jnp.float32)
    onsite = symmetric(diag_blocks[0, 0]) + levels[0, 0][:, None] * identity
    coup_x = x_coupling[0, 0] * flag_x
    coup_y = y_coupling[0, 0] * flag_y
    nbr_diag, nbr_coup = neighbour_blocks(onsite, coup_x, coup_y)
    columns = density_column(assemble(onsite, nbr_diag, nbr_coup))
    diag_one, x_one, y_one = averaged(columns)
    onsite_two = onsite + hubbard * (diag_one - 0.5 * identity)
    coup_x_two = coup_x + hubbard * x_one
    coup_y_two = coup_y + hubbard * y_one
    nbr_diag_two, nbr_coup_two = neighbour_blocks(onsite_two, coup_x_two, coup_y_two)
    columns_two = density_column(assemble(onsite_two, nbr_diag_two, nbr_coup_two))
    diag_two, x_two, y_two = averaged(columns_two)
    return (diag_two[None, None], x_two[None, None], y_two[None, None])


def solution(mesh):
    return jax.shard_map(
        per_device,
        mesh=mesh,
        in_specs=(
            P("space", "grp", None, None),
            P("space", "grp", None, None),
            P("space", "grp", None, None),
            P("space", "grp", None),
            P("space", "grp", None),
        ),
        out_specs=(
            P("space", "grp", None, None),
            P("space", "grp", None, None),
            P("space", "grp", None, None),
        ),
        check_vma=False,
    )
```

profile of v0, /device:TPU:23, one launch (start us, length us, event | category | flops | bytes accessed | tf_op | source)
XLA Modules:
  0.0 73.3 jit_solution(13647696412076590893)
XLA Ops:
  0.6 0.0 copy-start.2
  0.6 0.0 copy-start.3
  0.7 1.3 %fusion.68 = (s32[1,1,1]{2,1,0:T(1,128)}, s32[1,1,1]{2,1,0:T(1,128)}) fusion(s32[1,1,2]{2,1,0:T(1,128)} %param.9), kind=kLoop, calls=%fused_computation.122 | loop fusion | bytes 16 | tf_op jit(solution)/shard_map/slice | solution.py:80
  3.3 0.9 %copy.8 = f32[1,1,128,128]{2,3,1,0:T(8,128)S(1)} copy(f32[1,1,128,128]{3,2,1,0:T(8,128)} %param.5) | data formatting | bytes 131072 | tf_op args[0]
  4.2 0.9 %constant_dynamic-update-slice_fusion.2 = (f32[640,640]{1,0:T(8,128)S(1)}, f32[128,128]{1,0:T(8,128)S(1)}) fusion(f32[128]{0:T(128)} %bitcast.116, f32[1,1,128,128]{2,3,1,0:T(8,128)S(1)} %copy.8, f32[1,1,128,128]{3,2,1,0:T(8,128)} %param.5), kind=kLoop, calls=%fused_computation.111 | loop fusion | flops 81919 | bytes 262656
  5.2 0.9 %multiply_bitcast_fusion = (f32[128,128]{0,1:T(8,128)S(1)}, f32[1,128,128]{2,1,0:T(8,128)S(1)}, f32[1,128,128]{2,1,0:T(8,128)S(1)}, f32[128,128]{0,1:T(8,128)S(1)}) fusion(f32[1,1,128,128]{3,2,1,0:T(8,128)} %param.7, f32[]{:T(128)S(6)} %mul.123, f32[1,1,128,128]{3,2,1,0:T(8,128)} %param.6, f32[]{:T(128)S(6)} %mul.118), kind=kLoop, calls=%fused_computation.105 | loop fusion | flops 32768 | bytes 393224 | tf_op jit(solution)/shard_map/transpose | solution.py:62
  6.1 3.7 %collective-permute-start = (f32[2,128,128]{2,1,0:T(8,128)S(1)}, f32[2,128,128]{2,1,0:T(8,128)S(1)}, u32[]{:S(2)}, u32[]{:S(2)}) collective-permute-start(f32[2,128,128]{2,1,0:T(8,128)S(1)} %get-tuple-element.35), channel_id=1, source_target_pairs={{0,2},{2,4},{4,6},{6,8},{8,10},{10,12},{12,14},{14,16},{16,18},{18... | collective-permute-start | bytes 393224 | tf_op jit(solution)/shard_map/ppermute | solution.py:12
  9.8 1.9 %collective-permute-start.2 = (f32[128,128]{1,0:T(8,128)S(1)}, f32[128,128]{1,0:T(8,128)S(1)}, u32[]{:S(2)}, u32[]{:S(2)}) collective-permute-start(f32[128,128]{1,0:T(8,128)S(1)} %get-tuple-element.6), channel_id=1, source_target_pairs={{2,0},{4,2},{6,4},{8,6},{10,8},{12,10},{14,12},{16,14},{18,16},{20... | collective-permute-start | bytes 196616 | tf_op jit(solution)/shard_map/ppermute | solution.py:12
  11.7 2.2 %collective-permute-start.3 = (f32[128,128]{1,0:T(8,128)S(1)}, f32[128,128]{1,0:T(8,128)S(1)}, u32[]{:S(2)}, u32[]{:S(2)}) collective-permute-start(f32[128,128]{1,0:T(8,128)S(1)} %get-tuple-element.6), channel_id=1, source_target_pairs={{1,0},{3,2},{5,4},{7,6},{9,8},{11,10},{13,12},{15,14},{17,16},{19,... | collective-permute-start | bytes 196616 | tf_op jit(solution)/shard_map/ppermute | solution.py:12
  13.9 1.3 %collective-permute-start.1 = (f32[2,128,128]{2,1,0:T(8,128)S(1)}, f32[2,128,128]{2,1,0:T(8,128)S(1)}, u32[]{:S(2)}, u32[]{:S(2)}) collective-permute-start(f32[2,128,128]{2,1,0:T(8,128)S(1)} %get-tuple-element.34), channel_id=1, source_target_pairs={{0,1},{2,3},{4,5},{6,7},{8,9},{10,11},{12,13},{14,15},{16,17},{18,... | collective-permute-start | bytes 393224 | tf_op jit(solution)/shard_map/ppermute | solution.py:12
  15.2 0.1 copy.12
  15.3 0.1 copy.13
  15.4 0.1 iota_compare_fusion
  15.5 0.0 collective-permute-done
  15.6 0.1 copy.10
  15.7 0.0 copy-done.2
  15.7 4.3 %collective-permute-done.1 = f32[2,128,128]{2,1,0:T(8,128)S(1)} collective-permute-done((f32[2,128,128]{2,1,0:T(8,128)S(1)}, f32[2,128,128]{2,1,0:T(8,128)S(1)}, u32[]{:S(2)}, u32[]{:S(2)}) %collective-permute-start.1) | collective-permute-done | bytes 131104 | tf_op jit(solution)/shard_map/ppermute | solution.py:12
  20.0 0.1 copy.11
  20.1 0.0 copy-done.3
  20.2 0.0 collective-permute-done.2
  20.3 0.0 collective-permute-done.3
  20.3 0.9 %fusion.22 = f32[640,640]{1,0:T(8,128)S(1)} fusion(f32[640,640]{1,0:T(8,128)S(1)} %fusion.41), kind=kOutput, calls=%fused_computation.33 | convolution fusion | flops 524697600 | bytes 3276800 | tf_op jit(solution)/shard_map/dot_general | solution.py:36
  21.2 0.0 copy-start.1
  21.2 1.2 %copy-done.1 = f32[640,640]{1,0:T(8,128)} copy-done((f32[640,640]{1,0:T(8,128)}, f32[640,640]{1,0:T(8,128)S(1)}, u32[]{:S(2)}) %copy-start.1) | copy-done | bytes 1638424
  22.4 1.5 %fusion.24 = f32[]{:T(128)} fusion(f32[640,640]{1,0:T(8,128)S(1)} %fusion.22), kind=kOutput, calls=%fused_computation.35 | convolution fusion | flops 525516800 | bytes 1638404 | tf_op jit(solution)/shard_map/dot_general | solution.py:38
  24.7 3.2 %multiply_convert_fusion.1 = bf16[640,640]{1,0:T(8,128)(2,1)} fusion(f32[640,640]{1,0:T(8,128)S(1)} %fusion.41, f32[640,640]{1,0:T(8,128)} %copy-done.1, f32[]{:T(128)S(6)} %sqrt.19, f32[]{:T(128)S(6)} %sqrt.20), kind=kOutput, calls=%fused_computation.8 | convolution fusion | flops 527974400 | bytes 4096008 | tf_op jit(solution)/shard_map/dot_general | solution.py:45
  28.0 2.5 %fusion.4 = f32[640,128]{1,0:T(8,128)S(1)} fusion(bf16[640,640]{1,0:T(8,128)(2,1)} %multiply_convert_fusion.1, pred[640,640]{1,0:T(32,128)(4,1)S(1)} %iota_compare_fusion), kind=kOutput, calls=%fused_computation.15 | convolution fusion | flops 210370560 | bytes 2375680 | tf_op jit(solution)/shard_map/dot_general | solution.py:50
  30.5 0.1 copy.16
  30.6 3.7 %collective-permute-start.4 = (f32[128,128]{1,0:T(8,128)S(1)}, f32[128,128]{1,0:T(8,128)S(1)}, u32[]{:S(2)}, u32[]{:S(2)}) collective-permute-start(f32[128,128]{1,0:T(8,128)S(1)} %get-tuple-element.14), channel_id=1, source_target_pairs={{2,0},{4,2},{6,4},{8,6},{10,8},{12,10},{14,12},{16,14},{18,16},{20... | collective-permute-start | bytes 196616 | tf_op jit(solution)/shard_map/ppermute | solution.py:12
  34.3 0.1 copy.17
  34.4 1.3 %collective-permute-start.6 = (f32[128,128]{1,0:T(8,128)S(1)}, f32[128,128]{1,0:T(8,128)S(1)}, u32[]{:S(2)}, u32[]{:S(2)}) collective-permute-start(f32[128,128]{1,0:T(8,128)S(1)} %get-tuple-element.13), channel_id=1, source_target_pairs={{1,0},{3,2},{5,4},{7,6},{9,8},{11,10},{13,12},{15,14},{17,16},{19,... | collective-permute-start | bytes 196616 | tf_op jit(solution)/shard_map/ppermute | solution.py:12
  35.7 0.1 copy.30
  35.8 2.4 %collective-permute-done.4 = f32[128,128]{1,0:T(8,128)S(1)} collective-permute-done((f32[128,128]{1,0:T(8,128)S(1)}, f32[128,128]{1,0:T(8,128)S(1)}, u32[]{:S(2)}, u32[]{:S(2)}) %collective-permute-start.4) | collective-permute-done | bytes 65568 | tf_op jit(solution)/shard_map/ppermute | solution.py:12
  38.2 0.0 collective-permute-done.6
  38.3 3.6 %collective-permute-start.5 = (f32[2,128,128]{2,1,0:T(8,128)S(1)}, f32[2,128,128]{2,1,0:T(8,128)S(1)}, u32[]{:S(2)}, u32[]{:S(2)}) collective-permute-start(f32[2,128,128]{2,1,0:T(8,128)S(1)} %get-tuple-element.29), channel_id=1, source_target_pairs={{0,2},{2,4},{4,6},{6,8},{8,10},{10,12},{12,14},{14,16},{16,18},{18... | collective-permute-start | bytes 393224 | tf_op jit(solution)/shard_map/ppermute | solution.py:12
  41.9 1.9 %collective-permute-start.8 = (f32[128,128]{1,0:T(8,128)S(1)}, f32[128,128]{1,0:T(8,128)}, u32[]{:S(2)}, u32[]{:S(2)}) collective-permute-start(f32[128,128]{1,0:T(8,128)S(1)} %get-tuple-element.4), channel_id=1, source_target_pairs={{2,0},{4,2},{6,4},{8,6},{10,8},{12,10},{14,12},{16,14},{18,16},{20... | collective-permute-start | bytes 196616 | tf_op jit(solution)/shard_map/ppermute | solution.py:12
  43.8 4.1 %collective-permute-start.9 = (f32[128,128]{1,0:T(8,128)S(1)}, f32[128,128]{1,0:T(8,128)S(1)}, u32[]{:S(2)}, u32[]{:S(2)}) collective-permute-start(f32[128,128]{1,0:T(8,128)S(1)} %get-tuple-element.4), channel_id=1, source_target_pairs={{1,0},{3,2},{5,4},{7,6},{9,8},{11,10},{13,12},{15,14},{17,16},{19,... | collective-permute-start | bytes 196616 | tf_op jit(solution)/shard_map/ppermute | solution.py:12
  47.9 1.3 %collective-permute-start.7 = (f32[2,128,128]{2,1,0:T(8,128)S(1)}, f32[2,128,128]{2,1,0:T(8,128)S(1)}, u32[]{:S(2)}, u32[]{:S(2)}) collective-permute-start(f32[2,128,128]{2,1,0:T(8,128)S(1)} %get-tuple-element.28), channel_id=1, source_target_pairs={{0,1},{2,3},{4,5},{6,7},{8,9},{10,11},{12,13},{14,15},{16,17},{18,... | collective-permute-start | bytes 393224 | tf_op jit(solution)/shard_map/ppermute | solution.py:12
  49.2 0.1 copy.21
  49.3 0.1 copy.22
  49.4 0.0 collective-permute-done.5
  49.5 0.1 copy.19
  49.6 5.2 %collective-permute-done.7 = f32[2,128,128]{2,1,0:T(8,128)S(1)} collective-permute-done((f32[2,128,128]{2,1,0:T(8,128)S(1)}, f32[2,128,128]{2,1,0:T(8,128)S(1)}, u32[]{:S(2)}, u32[]{:S(2)}) %collective-permute-start.7) | collective-permute-done | bytes 131104 | tf_op jit(solution)/shard_map/ppermute | solution.py:12
  54.9 0.1 copy.20
  55.0 0.0 collective-permute-done.8
  55.0 0.9 %fusion.35 = f32[640,640]{1,0:T(8,128)S(1)} fusion(f32[640,640]{1,0:T(8,128)S(1)} %fusion.31, f32[128,256]{1,0:T(8,128)S(1)} %broadcast.56, f32[128,128]{1,0:T(8,128)S(1)} %broadcast.54, f32[128,128]{1,0:T(8,128)} %collective-permute-done.8, f32[128,128]{1,0:T(8,128)S(1)} %copy.21), kind=kLoop, calls=%fused_computation.54 | loop fusion | flops 245760 | bytes 655360
  55.9 0.0 collective-permute-done.9
  56.0 0.9 %fusion.13 = f32[640,640]{1,0:T(8,128)S(1)} fusion(f32[640,640]{1,0:T(8,128)S(1)} %fusion.43), kind=kOutput, calls=%fused_computation.24 | convolution fusion | flops 524697600 | bytes 3276800 | tf_op jit(solution)/shard_map/dot_general | solution.py:36
  56.9 0.0 copy-start
  56.9 1.2 %copy-done = f32[640,640]{1,0:T(8,128)} copy-done((f32[640,640]{1,0:T(8,128)}, f32[640,640]{1,0:T(8,128)S(1)}, u32[]{:S(2)}) %copy-start) | copy-done | bytes 1638424
  58.0 1.5 %fusion.27 = f32[]{:T(128)} fusion(f32[640,640]{1,0:T(8,128)S(1)} %fusion.13), kind=kOutput, calls=%fused_computation.36 | convolution fusion | flops 525516800 | bytes 1638404 | tf_op jit(solution)/shard_map/dot_general | solution.py:38
  60.4 2.3 %multiply_convert_fusion = bf16[640,640]{1,0:T(8,128)(2,1)S(1)} fusion(f32[640,640]{1,0:T(8,128)S(1)} %fusion.43, f32[640,640]{1,0:T(8,128)} %copy-done, f32[]{:T(128)S(6)} %sqrt.22, f32[]{:T(128)S(6)} %sqrt.23), kind=kOutput, calls=%fused_computation.6 | convolution fusion | flops 527974400 | bytes 4096008 | tf_op jit(solution)/shard_map/dot_general | solution.py:45
  62.7 0.9 %fusion.7 = f32[640,128]{1,0:T(8,128)S(1)} fusion(bf16[640,640]{1,0:T(8,128)(2,1)S(1)} %multiply_convert_fusion, pred[640,640]{1,0:T(32,128)(4,1)S(1)} %iota_compare_fusion), kind=kOutput, calls=%fused_computation.18 | convolution fusion | flops 210370560 | bytes 2375680 | tf_op jit(solution)/shard_map/dot_general | solution.py:50
  63.6 0.1 copy.31
  63.7 0.7 fusion.67
  64.3 1.3 %collective-permute-start.11 = (f32[128,128]{1,0:T(8,128)S(1)}, f32[128,128]{1,0:T(8,128)S(1)}, u32[]{:S(2)}, u32[]{:S(2)}) collective-permute-start(f32[128,128]{1,0:T(8,128)S(1)} %get-tuple-element.11), channel_id=1, source_target_pairs={{1,0},{3,2},{5,4},{7,6},{9,8},{11,10},{13,12},{15,14},{17,16},{19,... | collective-permute-start | bytes 196616 | tf_op jit(solution)/shard_map/ppermute | solution.py:12
  65.6 0.1 copy.33
  65.7 3.0 %collective-permute-start.10 = (f32[128,128]{1,0:T(8,128)S(1)}, f32[128,128]{1,0:T(8,128)S(1)}, u32[]{:S(2)}, u32[]{:S(2)}) collective-permute-start(f32[128,128]{1,0:T(8,128)S(1)} %get-tuple-element.10), channel_id=1, source_target_pairs={{2,0},{4,2},{6,4},{8,6},{10,8},{12,10},{14,12},{16,14},{18,16},{20... | collective-permute-start | bytes 196616 | tf_op jit(solution)/shard_map/ppermute | solution.py:12
  68.7 0.1 copy.32
  68.8 0.0 collective-permute-done.11
  68.8 0.6 fusion.51
  69.4 3.2 %collective-permute-done.10 = f32[128,128]{1,0:T(8,128)S(1)} collective-permute-done((f32[128,128]{1,0:T(8,128)S(1)}, f32[128,128]{1,0:T(8,128)S(1)}, u32[]{:S(2)}, u32[]{:S(2)}) %collective-permute-start.10) | collective-permute-done | bytes 65568 | tf_op jit(solution)/shard_map/ppermute | solution.py:12
  72.6 0.6 fusion.53
  (29 shorter events, 0.4 us)
Async XLA Ops:
  0.6 15.1 %copy-start.2 = (f32[1,1,128,128]{3,2,1,0:T(8,128)S(1)}, f32[1,1,128,128]{3,2,1,0:T(8,128)}, u32[]{:S(2)}) copy-start(f32[1,1,128,128]{3,2,1,0:T(8,128)} %param.6) | copy-start | bytes 196612
  0.6 19.5 %copy-start.3 = (f32[1,1,128,128]{3,2,1,0:T(8,128)S(1)}, f32[1,1,128,128]{3,2,1,0:T(8,128)}, u32[]{:S(2)}) copy-start(f32[1,1,128,128]{3,2,1,0:T(8,128)} %param.7) | copy-start | bytes 196612
  6.1 9.4 %collective-permute-start = (f32[2,128,128]{2,1,0:T(8,128)S(1)}, f32[2,128,128]{2,1,0:T(8,128)S(1)}, u32[]{:S(2)}, u32[]{:S(2)}) collective-permute-start(f32[2,128,128]{2,1,0:T(8,128)S(1)} %get-tuple-element.35), channel_id=1, source_target_pairs={{0,2},{2,4},{4,6},{6,8},{8,10},{10,12},{12,14},{14,16},{16,18},{18... | collective-permute-start | bytes 393224 | tf_op jit(solution)/shard_map/ppermute | solution.py:12
  9.8 10.4 %collective-permute-start.2 = (f32[128,128]{1,0:T(8,128)S(1)}, f32[128,128]{1,0:T(8,128)S(1)}, u32[]{:S(2)}, u32[]{:S(2)}) collective-permute-start(f32[128,128]{1,0:T(8,128)S(1)} %get-tuple-element.6), channel_id=1, source_target_pairs={{2,0},{4,2},{6,4},{8,6},{10,8},{12,10},{14,12},{16,14},{18,16},{20... | collective-permute-start | bytes 196616 | tf_op jit(solution)/shard_map/ppermute | solution.py:12
  11.7 8.6 %collective-permute-start.3 = (f32[128,128]{1,0:T(8,128)S(1)}, f32[128,128]{1,0:T(8,128)S(1)}, u32[]{:S(2)}, u32[]{:S(2)}) collective-permute-start(f32[128,128]{1,0:T(8,128)S(1)} %get-tuple-element.6), channel_id=1, source_target_pairs={{1,0},{3,2},{5,4},{7,6},{9,8},{11,10},{13,12},{15,14},{17,16},{19,... | collective-permute-start | bytes 196616 | tf_op jit(solution)/shard_map/ppermute | solution.py:12
  13.9 6.1 %collective-permute-start.1 = (f32[2,128,128]{2,1,0:T(8,128)S(1)}, f32[2,128,128]{2,1,0:T(8,128)S(1)}, u32[]{:S(2)}, u32[]{:S(2)}) collective-permute-start(f32[2,128,128]{2,1,0:T(8,128)S(1)} %get-tuple-element.34), channel_id=1, source_target_pairs={{0,1},{2,3},{4,5},{6,7},{8,9},{10,11},{12,13},{14,15},{16,17},{18,... | collective-permute-start | bytes 393224 | tf_op jit(solution)/shard_map/ppermute | solution.py:12
  21.2 1.2 %copy-start.1 = (f32[640,640]{1,0:T(8,128)}, f32[640,640]{1,0:T(8,128)S(1)}, u32[]{:S(2)}) copy-start(f32[640,640]{1,0:T(8,128)S(1)} %fusion.22) | copy-start | bytes 4915204
  30.6 7.6 %collective-permute-start.4 = (f32[128,128]{1,0:T(8,128)S(1)}, f32[128,128]{1,0:T(8,128)S(1)}, u32[]{:S(2)}, u32[]{:S(2)}) collective-permute-start(f32[128,128]{1,0:T(8,128)S(1)} %get-tuple-element.14), channel_id=1, source_target_pairs={{2,0},{4,2},{6,4},{8,6},{10,8},{12,10},{14,12},{16,14},{18,16},{20... | collective-permute-start | bytes 196616 | tf_op jit(solution)/shard_map/ppermute | solution.py:12
  34.4 3.8 %collective-permute-start.6 = (f32[128,128]{1,0:T(8,128)S(1)}, f32[128,128]{1,0:T(8,128)S(1)}, u32[]{:S(2)}, u32[]{:S(2)}) collective-permute-start(f32[128,128]{1,0:T(8,128)S(1)} %get-tuple-element.13), channel_id=1, source_target_pairs={{1,0},{3,2},{5,4},{7,6},{9,8},{11,10},{13,12},{15,14},{17,16},{19,... | collective-permute-start | bytes 196616 | tf_op jit(solution)/shard_map/ppermute | solution.py:12
  38.3 11.2 %collective-permute-start.5 = (f32[2,128,128]{2,1,0:T(8,128)S(1)}, f32[2,128,128]{2,1,0:T(8,128)S(1)}, u32[]{:S(2)}, u32[]{:S(2)}) collective-permute-start(f32[2,128,128]{2,1,0:T(8,128)S(1)} %get-tuple-element.29), channel_id=1, source_target_pairs={{0,2},{2,4},{4,6},{6,8},{8,10},{10,12},{12,14},{14,16},{16,18},{18... | collective-permute-start | bytes 393224 | tf_op jit(solution)/shard_map/ppermute | solution.py:12
  41.9 13.1 %collective-permute-start.8 = (f32[128,128]{1,0:T(8,128)S(1)}, f32[128,128]{1,0:T(8,128)}, u32[]{:S(2)}, u32[]{:S(2)}) collective-permute-start(f32[128,128]{1,0:T(8,128)S(1)} %get-tuple-element.4), channel_id=1, source_target_pairs={{2,0},{4,2},{6,4},{8,6},{10,8},{12,10},{14,12},{16,14},{18,16},{20... | collective-permute-start | bytes 196616 | tf_op jit(solution)/shard_map/ppermute | solution.py:12
  43.8 12.1 %collective-permute-start.9 = (f32[128,128]{1,0:T(8,128)S(1)}, f32[128,128]{1,0:T(8,128)S(1)}, u32[]{:S(2)}, u32[]{:S(2)}) collective-permute-start(f32[128,128]{1,0:T(8,128)S(1)} %get-tuple-element.4), channel_id=1, source_target_pairs={{1,0},{3,2},{5,4},{7,6},{9,8},{11,10},{13,12},{15,14},{17,16},{19,... | collective-permute-start | bytes 196616 | tf_op jit(solution)/shard_map/ppermute | solution.py:12
  47.9 6.9 %collective-permute-start.7 = (f32[2,128,128]{2,1,0:T(8,128)S(1)}, f32[2,128,128]{2,1,0:T(8,128)S(1)}, u32[]{:S(2)}, u32[]{:S(2)}) collective-permute-start(f32[2,128,128]{2,1,0:T(8,128)S(1)} %get-tuple-element.28), channel_id=1, source_target_pairs={{0,1},{2,3},{4,5},{6,7},{8,9},{10,11},{12,13},{14,15},{16,17},{18,... | collective-permute-start | bytes 393224 | tf_op jit(solution)/shard_map/ppermute | solution.py:12
  56.9 1.2 %copy-start = (f32[640,640]{1,0:T(8,128)}, f32[640,640]{1,0:T(8,128)S(1)}, u32[]{:S(2)}) copy-start(f32[640,640]{1,0:T(8,128)S(1)} %fusion.13) | copy-start | bytes 4915204
  64.3 4.5 %collective-permute-start.11 = (f32[128,128]{1,0:T(8,128)S(1)}, f32[128,128]{1,0:T(8,128)S(1)}, u32[]{:S(2)}, u32[]{:S(2)}) collective-permute-start(f32[128,128]{1,0:T(8,128)S(1)} %get-tuple-element.11), channel_id=1, source_target_pairs={{1,0},{3,2},{5,4},{7,6},{9,8},{11,10},{13,12},{15,14},{17,16},{19,... | collective-permute-start | bytes 196616 | tf_op jit(solution)/shard_map/ppermute | solution.py:12
  65.7 6.9 %collective-permute-start.10 = (f32[128,128]{1,0:T(8,128)S(1)}, f32[128,128]{1,0:T(8,128)S(1)}, u32[]{:S(2)}, u32[]{:S(2)}) collective-permute-start(f32[128,128]{1,0:T(8,128)S(1)} %get-tuple-element.10), channel_id=1, source_target_pairs={{2,0},{4,2},{6,4},{8,6},{10,8},{12,10},{14,12},{16,14},{18,16},{20... | collective-permute-start | bytes 196616 | tf_op jit(solution)/shard_map/ppermute | solution.py:12
where the time goes:
time: 74 us; the launch traced here: 73.3 us
  starting transfers between devices  29.2 us (39%)
  waiting for transfers between devices  15.1 us (20%)
  matrix products  13.7 us (19%)
  local copies, waits for them, and re-layouts  6.01 us (8%)
  other arithmetic  5.06 us (7%)
  between operations  4.11 us (6%)
    ppermute x12, starting transfers between devices, shifted(): return lax.ppermute(x, axis, pairs)  29.2 us
    ppermute x12, waiting for transfers between devices, shifted(): return lax.ppermute(x, axis, pairs)  15.1 us
    dot_general x2, matrix products, density_column(): jnp.dot(initial, factor, preferred_element_type=jnp.float32)  5.55 us
    unnamed x19, local copies, waits for them, and re-layouts  3.7 us
    dot_general x2, matrix products, density_column(): jnp.dot(iterate, applied_once, preferred_element_type=jnp.float32)  3.36 us
    dot_general x2, matrix products, density_column(): jnp.dot(square_half, square_half, preferred_element_type=jnp.float32)  3.07 us
    unnamed x10, other arithmetic  1.98 us
    dot_general x2, matrix products, density_column(): jnp.dot(matrix_half, matrix_half, preferred_element_type=jnp.float32)  1.75 us
  transfers between devices with their start and end apart: 12, of which 4 were waited for; matrix products, arithmetic and copies ran while one was open for 4% of the time, Pallas kernels for 0%

commit v1 on v0

v1 whole, which is shorter than its diff:
```python
import functools

import jax
import jax.numpy as jnp
from jax import lax
from jax.experimental import pallas as pl
from jax.experimental.pallas import tpu as pltpu
from jax.sharding import PartitionSpec as P

hubbard = 1.0
MESH = pl.DeviceIdType.MESH
F32 = jnp.float32
BF16 = jnp.bfloat16


def mm(a, b):
    return jnp.dot(a, b, preferred_element_type=F32)


def eye(w):
    return lax.broadcasted_iota(jnp.int32, (w, w), 0) == lax.broadcasted_iota(jnp.int32, (w, w), 1)


def density_columns(w, row0, v1, dk, sx, fb, w13, v3, v5, v7, v5b, v1f, cols):
    n = 5 * w

    def bl(i):
        return slice(i * w, (i + 1) * w)

    d0 = row0[:, bl(0)]
    sx[:, n:] = v1[...]
    w13[:, :w] = v1[...]
    sx[bl(0), bl(0)] = mm(row0[...], v1[...]).astype(BF16)
    for half in range(2):
        t = mm(v1[w:, :], row0[:, w * (1 + 2 * half) : w * (3 + 2 * half)])
        for l in (0, 1):
            k = 2 * half + l
            for r in range(4):
                piece = t[bl(r), bl(l)]
                if r == k:
                    piece = piece + mm(dk[k], dk[k])
                sx[bl(1 + r), bl(1 + k)] = piece.astype(BF16)
    for k in range(4):
        bk, btk = v1[bl(1 + k), :], row0[:, bl(1 + k)]
        sx[bl(1 + k), bl(0)] = (mm(bk, d0) + mm(dk[k], bk)).astype(BF16)
        sx[bl(0), bl(1 + k)] = (mm(d0, btk) + mm(btk, dk[k])).astype(BF16)
    total = jnp.zeros((1, 2 * w), F32)
    for c in range(3):
        f = mm(sx[:, :n], sx[:, 2 * w * c : 2 * w * (c + 1)])
        if c == 2:
            v3[...] = f[:, w:]
            w13[:, w:] = f[:, w:].astype(BF16)
            f = f[:, :w]
            fb[:, 4 * w :] = f.astype(BF16)
            last = jnp.sum(f * f, axis=0, keepdims=True)
        else:
            fb[:, 2 * w * c : 2 * w * (c + 1)] = f.astype(BF16)
            total = total + jnp.sum(f * f, axis=0, keepdims=True)
    g = mm(fb[...], w13[...])
    v5[...] = g[:, :w]
    v5b[...] = g[:, :w].astype(BF16)
    v7[...] = g[:, w:]
    v9 = mm(fb[...], v5b[...])
    squares = jnp.sum(total, axis=1, keepdims=True) + jnp.sum(last, axis=1, keepdims=True)
    scale_two = jnp.sqrt(jnp.sqrt(squares + 1e-06))
    scale_one = jnp.sqrt(scale_two)
    al = 1.5 / scale_one
    be = 0.5 / (scale_one * scale_two)
    c1 = -0.75 * al
    c3 = 0.75 * be + 0.25 * al * al * al
    c5 = -0.75 * al * al * be
    c7 = 0.75 * al * be * be
    c9 = -0.25 * be * be * be
    res = c1 * v1f[...] + c3 * v3[...] + c5 * v5[...] + c7 * v7[...] + c9 * v9
    cols[...] = res
    cols[bl(0), :] = res[bl(0), :] + jnp.where(eye(w), 0.5, 0.0)


def kernel(
    sizes, diag_hbm, x_hbm, y_hbm, lev_hbm, list_hbm, od_ref, ox_ref, oy_ref,
    din, xin, yin, lin, fin, in_sems,
    send1, rd1, rb1, send2, rd2, rc2, rf3,
    row0, v1, dk, sx, fb, w13, v3, v5, v7, v5b, v1f, cols,
    send_sems, recv_sems,
):
    nx, ny = sizes
    w = din.shape[0]
    ix = lax.axis_index("space")
    iy = lax.axis_index("grp")
    has = [ix > 0, ix < nx - 1, iy > 0, iy < ny - 1]
    dev = [
        (jnp.maximum(ix - 1, 0), iy),
        (jnp.minimum(ix + 1, nx - 1), iy),
        (ix, jnp.maximum(iy - 1, 0)),
        (ix, jnp.minimum(iy + 1, ny - 1)),
    ]

    def bl(i):
        return slice(i * w, (i + 1) * w)

    barrier = pltpu.get_barrier_semaphore()
    for k in range(4):
        @pl.when(has[k])
        def _():
            pl.semaphore_signal(barrier, inc=1, device_id=dev[k], device_id_type=MESH)

    loads = [
        pltpu.make_async_copy(diag_hbm.at[0, 0], din, in_sems.at[0]),
        pltpu.make_async_copy(x_hbm.at[0, 0], xin, in_sems.at[1]),
        pltpu.make_async_copy(y_hbm.at[0, 0], yin, in_sems.at[2]),
        pltpu.make_async_copy(lev_hbm.at[0], lin, in_sems.at[3]),
        pltpu.make_async_copy(list_hbm.at[0], fin, in_sems.at[4]),
    ]
    for load in loads:
        load.start()
    for k in range(4):
        @pl.when(jnp.logical_not(has[k]))
        def _():
            zero = jnp.zeros((w, w), F32)
            rd1[k] = zero
            rd2[k] = zero
            rc2[k] = zero
            if k % 2 == 0:
                rb1[k // 2] = zero
            else:
                rf3[k // 2] = zero
    for load in loads:
        load.wait()
    one_eye = eye(w)
    flag_x = fin[0, 0].astype(F32) * (ix < nx - 1).astype(F32)
    flag_y = fin[0, 1].astype(F32) * (iy < ny - 1).astype(F32)
    raw = din[...]
    onsite = 0.5 * (raw + raw.T) + jnp.where(one_eye, jnp.broadcast_to(lin[...], (w, w)), 0.0)
    send1[0] = onsite
    send1[1] = xin[...] * flag_x
    send1[2] = yin[...] * flag_y

    count = sum(h.astype(jnp.int32) for h in has)
    pl.semaphore_wait(barrier, count)

    def transfer(src, dst, index_send, index_recv, k):
        return pltpu.make_async_remote_copy(
            src_ref=src, dst_ref=dst, send_sem=send_sems.at[index_send],
            recv_sem=recv_sems.at[index_recv], device_id=dev[k], device_id_type=MESH,
        )

    def diag1(k):
        return transfer(send1.at[0], rd1.at[k ^ 1], k, k ^ 1, k)

    def coup1(k):
        return transfer(send1.at[1 + k // 2], rb1.at[k // 2], 4 + k // 2, 4 + k // 2, k)

    def diag2(k):
        return transfer(send2, rd2.at[k ^ 1], 6 + k, 6 + (k ^ 1), k)

    def coup2(k):
        return transfer(cols1.at[bl(1 + k), :], rc2.at[k ^ 1], 10 + k, 10 + (k ^ 1), k)

    def coup3(k):
        return transfer(cols2.at[bl(1 + k), :], rf3.at[k // 2], 14 + k // 2, 14 + k // 2, k)

    cols1, cols2 = cols.at[0], cols.at[1]

    order = (3, 2, 1, 0)
    for k in order:
        @pl.when(has[k])
        def _():
            if k % 2:
                coup1(k).start()
            diag1(k).start()

    row0[:, bl(0)] = onsite.astype(BF16)
    v1[bl(0), :] = onsite.astype(BF16)
    v1f[bl(0), :] = onsite
    for axis in range(2):
        coup = send1[1 + axis]
        coup_t = coup.T
        row0[:, bl(2 + 2 * axis)] = coup.astype(BF16)
        v1[bl(2 + 2 * axis), :] = coup_t.astype(BF16)
        v1f[bl(2 + 2 * axis), :] = coup_t
    for k in (0, 1, 2, 3):
        @pl.when(has[k])
        def _():
            if k % 2 == 0:
                coup1(k ^ 1).wait_recv()
            diag1(k ^ 1).wait_recv()
    for k in range(4):
        dk[k] = rd1[k].astype(BF16)
    for axis in range(2):
        coup = rb1[axis]
        row0[:, bl(1 + 2 * axis)] = coup.T.astype(BF16)
        v1[bl(1 + 2 * axis), :] = coup.astype(BF16)
        v1f[bl(1 + 2 * axis), :] = coup

    density_columns(w, row0, v1, dk, sx, fb, w13, v3, v5, v7, v5b, v1f, cols1)

    for k in order:
        @pl.when(has[k])
        def _():
            coup2(k).start()
    c0 = cols1[bl(0), :]
    onsite_two = v1f[bl(0), :] + hubbard * (0.5 * (c0 + c0.T) - jnp.where(one_eye, 0.5, 0.0))
    send2[...] = onsite_two
    for k in order:
        @pl.when(has[k])
        def _():
            diag2(k).start()
    row0[:, bl(0)] = onsite_two.astype(BF16)
    v1[bl(0), :] = onsite_two.astype(BF16)
    v1f[bl(0), :] = onsite_two
    for k in range(4):
        v1f[bl(1 + k), :] = v1f[bl(1 + k), :] + 0.5 * hubbard * cols1[bl(1 + k), :]
    for k in (0, 1, 2, 3):
        @pl.when(has[k])
        def _():
            coup2(k ^ 1).wait_recv()
            diag2(k ^ 1).wait_recv()
    for k in range(4):
        dk[k] = rd2[k].astype(BF16)
        bk = v1f[bl(1 + k), :] + 0.5 * hubbard * rc2[k].T
        v1f[bl(1 + k), :] = bk
        v1[bl(1 + k), :] = bk.astype(BF16)
        row0[:, bl(1 + k)] = bk.T.astype(BF16)

    density_columns(w, row0, v1, dk, sx, fb, w13, v3, v5, v7, v5b, v1f, cols2)

    for k in (2, 0):
        @pl.when(has[k])
        def _():
            coup3(k).start()
    c0 = cols2[bl(0), :]
    od_ref[0, 0] = 0.5 * (c0 + c0.T)
    ox_ref[0, 0] = 0.5 * cols2[bl(2), :].T
    oy_ref[0, 0] = 0.5 * cols2[bl(4), :].T
    for k in (1, 3):
        @pl.when(has[k])
        def _():
            coup3(k ^ 1).wait_recv()
    ox_ref[0, 0] = ox_ref[0, 0] + 0.5 * rf3[0]
    oy_ref[0, 0] = oy_ref[0, 0] + 0.5 * rf3[1]
    for k in range(4):
        @pl.when(has[k])
        def _():
            if k % 2:
                coup1(k).wait_send()
            else:
                coup3(k).wait_send()
            diag1(k).wait_send()
            coup2(k).wait_send()
            diag2(k).wait_send()


def per_device(diag_blocks, x_coupling, y_coupling, levels, listed):
    w = diag_blocks.shape[-1]
    n = 5 * w
    sizes = (lax.axis_size("space"), lax.axis_size("grp"))
    block = jax.ShapeDtypeStruct((1, 1, w, w), F32)
    any_spec = pl.BlockSpec(memory_space=pl.ANY)
    vmem_spec = pl.BlockSpec(memory_space=pltpu.VMEM)
    return pl.pallas_call(
        functools.partial(kernel, sizes),
        out_shape=(block, block, block),
        in_specs=[any_spec] * 5,
        out_specs=(vmem_spec,) * 3,
        scratch_shapes=[
            pltpu.VMEM((w, w), F32),
            pltpu.VMEM((w, w), F32),
            pltpu.VMEM((w, w), F32),
            pltpu.VMEM((1, w), F32),
            pltpu.SMEM((1, 2), jnp.int32),
            pltpu.SemaphoreType.DMA((5,)),
            pltpu.VMEM((3, w, w), F32),
            pltpu.VMEM((4, w, w), F32),
            pltpu.VMEM((2, w, w), F32),
            pltpu.VMEM((w, w), F32),
            pltpu.VMEM((4, w, w), F32),
            pltpu.VMEM((4, w, w), F32),
            pltpu.VMEM((2, w, w), F32),
            pltpu.VMEM((w, n), BF16),
            pltpu.VMEM((n, w), BF16),
            pltpu.VMEM((4, w, w), BF16),
            pltpu.VMEM((n, n + w), BF16),
            pltpu.VMEM((n, n), BF16),
            pltpu.VMEM((n, 2 * w), BF16),
            pltpu.VMEM((n, w), F32),
            pltpu.VMEM((n, w), F32),
            pltpu.VMEM((n, w), F32),
            pltpu.VMEM((n, w), BF16),
            pltpu.VMEM((n, w), F32),
            pltpu.VMEM((2, n, w), F32),
            pltpu.SemaphoreType.DMA((16,)),
            pltpu.SemaphoreType.DMA((16,)),
        ],
        compiler_params=pltpu.CompilerParams(collective_id=0, has_side_effects=True),
    )(diag_blocks, x_coupling, y_coupling, levels, listed)


def solution(mesh):
    blocks = P("space", "grp", None, None)
    rows = P("space", "grp", None)
    return jax.shard_map(
        per_device,
        mesh=mesh,
        in_specs=(blocks, blocks, blocks, rows, rows),
        out_specs=(blocks, blocks, blocks),
        check_vma=False,
    )
```

time: 74 us -> 25.8 us (0.35)
  the two profiles are of different devices: /device:TPU:23 before, /device:TPU:0 now
where the time goes in v1:
time: 25.8 us; the launch traced here: 25.5 us
  Pallas kernels  21.8 us (84%)
  local copies, waits for them, and re-layouts  3 us (12%)
  between operations  0.65 us (3%)
    pallas_call x1, Pallas kernels, per_device(): pl.pallas_call(functools.partial(kernel, sizes), out_shape=(block, block,...  21.8 us
    unnamed x7, local copies, waits for them, and re-layouts  3 us

profile of v1, /device:TPU:0, one launch (start us, length us, event | category | flops | bytes accessed | tf_op | source)
XLA Modules:
  0.0 25.5 jit_solution(11980418053820155375)
XLA Ops:
  0.6 21.8 %shard_map.76 = (f32[1,1,128,128]{3,2,1,0:T(8,128)}, f32[1,1,128,128]{3,2,1,0:T(8,128)}, f32[1,1,128,128]{3,2,1,0:T(8,128)}) custom-call(f32[1,1,128,128]{3,2,1,0:T(8,128)} %diag_hbm.1, f32[1,1,128,128]{3,2,1,0:T(8,128)} %x_hbm.1, f32[1,1,128,128]{3,2,1,0:T(8,128)} %y_hbm.1, f32[1,1,128]{2,1,0:T(1,128)} %lev_hbm.1, s32[1,1,2]{2,1,0:T(1,128)} %list_hbm.1), custom_call_target="tpu_custom_call" | custom-call | tf_op jit(solution)/shard_map/pallas_call | solution.py:260
  22.5 0.0 copy-start.1
  22.5 1.5 %copy.11 = f32[1,1,128,128]{3,2,1,0:T(8,128)} copy(f32[1,1,128,128]{3,2,1,0:T(8,128)} %get-tuple-element.6) | data formatting | bytes 131072
  24.0 0.0 copy-done.1
  24.0 0.0 copy-start
  24.0 0.6 %copy.12 = f32[1,1,128,128]{3,2,1,0:T(8,128)} copy(f32[1,1,128,128]{3,2,1,0:T(8,128)S(1)} %copy-done.1) | data formatting | bytes 131072
  24.6 0.2 copy-done
  24.9 0.6 %copy.13 = f32[1,1,128,128]{3,2,1,0:T(8,128)} copy(f32[1,1,128,128]{3,2,1,0:T(8,128)S(1)} %copy-done) | data formatting | bytes 131072
Async XLA Ops:
  22.5 1.5 %copy-start.1 = (f32[1,1,128,128]{3,2,1,0:T(8,128)S(1)}, f32[1,1,128,128]{3,2,1,0:T(8,128)}, u32[]{:S(2)}) copy-start(f32[1,1,128,128]{3,2,1,0:T(8,128)} %get-tuple-element.7) | copy-start | bytes 196612
  24.0 0.9 %copy-start = (f32[1,1,128,128]{3,2,1,0:T(8,128)S(1)}, f32[1,1,128,128]{3,2,1,0:T(8,128)}, u32[]{:S(2)}) copy-start(f32[1,1,128,128]{3,2,1,0:T(8,128)} %get-tuple-element.8) | copy-start | bytes 196612

commit v2 on v1

--- a/solution.py
+++ b/solution.py
@@ -21,47 +21,49 @@
     return lax.broadcasted_iota(jnp.int32, (w, w), 0) == lax.broadcasted_iota(jnp.int32, (w, w), 1)
 
 
-def density_columns(w, row0, v1, dk, sx, fb, w13, v3, v5, v7, v5b, v1f, cols):
+def density_columns(w, row0, v1, dk, sx, fb, v3, u, v1f, cols, after_x, arrived):
     n = 5 * w
 
     def bl(i):
         return slice(i * w, (i + 1) * w)
 
     d0 = row0[:, bl(0)]
-    sx[:, n:] = v1[...]
-    w13[:, :w] = v1[...]
+    for k in arrived(range(4)):
+        top = jnp.concatenate([d0, row0[:, bl(1 + k)]], axis=1)
+        low = jnp.concatenate([v1[bl(1 + k), :], dk[k]], axis=1)
+        pair = jnp.concatenate([top, low], axis=0)
+        part = mm(pair, pair).astype(BF16)
+        sx[bl(0), bl(1 + k)] = part[:w, w:]
+        sx[bl(1 + k), bl(0)] = part[w:, :w]
+        sx[bl(1 + k), bl(1 + k)] = part[w:, w:]
     sx[bl(0), bl(0)] = mm(row0[...], v1[...]).astype(BF16)
     for half in range(2):
         t = mm(v1[w:, :], row0[:, w * (1 + 2 * half) : w * (3 + 2 * half)])
         for l in (0, 1):
             k = 2 * half + l
             for r in range(4):
-                piece = t[bl(r), bl(l)]
-                if r == k:
-                    piece = piece + mm(dk[k], dk[k])
-                sx[bl(1 + r), bl(1 + k)] = piece.astype(BF16)
-    for k in range(4):
-        bk, btk = v1[bl(1 + k), :], row0[:, bl(1 + k)]
-        sx[bl(1 + k), bl(0)] = (mm(bk, d0) + mm(dk[k], bk)).astype(BF16)
-        sx[bl(0), bl(1 + k)] = (mm(d0, btk) + mm(btk, dk[k])).astype(BF16)
+                if r != k:
+                    sx[bl(1 + r), bl(1 + k)] = t[bl(r), bl(l)].astype(BF16)
+    first = mm(row0[...], sx[:, bl(0)])
+    v3[bl(0), :] = first
+    sx[bl(0), n:] = first.astype(BF16)
+    for k in range(4):
+        low = jnp.concatenate([v1[bl(1 + k), :], dk[k]], axis=1)
+        vec = jnp.concatenate([sx[bl(0), bl(0)], sx[bl(1 + k), bl(0)]], axis=0)
+        first = mm(low, vec)
+        v3[bl(1 + k), :] = first
+        sx[bl(1 + k), n:] = first.astype(BF16)
     total = jnp.zeros((1, 2 * w), F32)
-    for c in range(3):
+    for c in range(2):
         f = mm(sx[:, :n], sx[:, 2 * w * c : 2 * w * (c + 1)])
-        if c == 2:
-            v3[...] = f[:, w:]
-            w13[:, w:] = f[:, w:].astype(BF16)
-            f = f[:, :w]
-            fb[:, 4 * w :] = f.astype(BF16)
-            last = jnp.sum(f * f, axis=0, keepdims=True)
-        else:
-            fb[:, 2 * w * c : 2 * w * (c + 1)] = f.astype(BF16)
-            total = total + jnp.sum(f * f, axis=0, keepdims=True)
-    g = mm(fb[...], w13[...])
-    v5[...] = g[:, :w]
-    v5b[...] = g[:, :w].astype(BF16)
-    v7[...] = g[:, w:]
-    v9 = mm(fb[...], v5b[...])
-    squares = jnp.sum(total, axis=1, keepdims=True) + jnp.sum(last, axis=1, keepdims=True)
+        fb[:, 2 * w * c : 2 * w * (c + 1)] = f.astype(BF16)
+        total = total + jnp.sum(f * f, axis=0, keepdims=True)
+    f = mm(sx[:, :n], sx[:, 4 * w :])
+    v5 = f[:, w:]
+    f = f[:, :w]
+    fb[:, 4 * w :] = f.astype(BF16)
+    total = total[:, :w] + total[:, w:] + jnp.sum(f * f, axis=0, keepdims=True)
+    squares = jnp.sum(total, axis=1, keepdims=True)
     scale_two = jnp.sqrt(jnp.sqrt(squares + 1e-06))
     scale_one = jnp.sqrt(scale_two)
     al = 1.5 / scale_one
@@ -71,16 +73,20 @@
     c5 = -0.75 * al * al * be
     c7 = 0.75 * al * be * be
     c9 = -0.25 * be * be * be
-    res = c1 * v1f[...] + c3 * v3[...] + c5 * v5[...] + c7 * v7[...] + c9 * v9
-    cols[...] = res
-    cols[bl(0), :] = res[bl(0), :] + jnp.where(eye(w), 0.5, 0.0)
+    u[...] = (c5 * v1f[...] + c7 * v3[...] + c9 * v5).astype(BF16)
+    top = slice(0, 3 * w)
+    cols[top, :] = mm(fb[top, :], u[...]) + (c1 * v1f[top, :] + c3 * v3[top, :])
+    cols[bl(0), :] = cols[bl(0), :] + jnp.where(eye(w), 0.5, 0.0)
+    after_x()
+    top = slice(3 * w, n)
+    cols[top, :] = mm(fb[top, :], u[...]) + (c1 * v1f[top, :] + c3 * v3[top, :])
 
 
 def kernel(
-    sizes, diag_hbm, x_hbm, y_hbm, lev_hbm, list_hbm, od_ref, ox_ref, oy_ref,
+    sizes, diag_hbm, x_hbm, y_hbm, lev_hbm, list_hbm, out_ref,
     din, xin, yin, lin, fin, in_sems,
     send1, rd1, rb1, send2, rd2, rc2, rf3,
-    row0, v1, dk, sx, fb, w13, v3, v5, v7, v5b, v1f, cols,
+    row0, v1, dk, sx, fb, v3, u, v1f, cols,
     send_sems, recv_sems,
 ):
     nx, ny = sizes
@@ -161,7 +167,7 @@
 
     cols1, cols2 = cols.at[0], cols.at[1]
 
-    order = (3, 2, 1, 0)
+    order = (1, 0, 3, 2)
     for k in order:
         @pl.when(has[k])
         def _():
@@ -178,66 +184,83 @@
         row0[:, bl(2 + 2 * axis)] = coup.astype(BF16)
         v1[bl(2 + 2 * axis), :] = coup_t.astype(BF16)
         v1f[bl(2 + 2 * axis), :] = coup_t
-    for k in (0, 1, 2, 3):
-        @pl.when(has[k])
-        def _():
+    def arrived1(slots):
+        for k in (2, 3, 1, 0):
+            @pl.when(has[k])
+            def _():
+                if k % 2 == 0:
+                    coup1(k ^ 1).wait_recv()
+                diag1(k ^ 1).wait_recv()
+            dk[k] = rd1[k].astype(BF16)
             if k % 2 == 0:
-                coup1(k ^ 1).wait_recv()
-            diag1(k ^ 1).wait_recv()
-    for k in range(4):
-        dk[k] = rd1[k].astype(BF16)
-    for axis in range(2):
-        coup = rb1[axis]
-        row0[:, bl(1 + 2 * axis)] = coup.T.astype(BF16)
-        v1[bl(1 + 2 * axis), :] = coup.astype(BF16)
-        v1f[bl(1 + 2 * axis), :] = coup
-
-    density_columns(w, row0, v1, dk, sx, fb, w13, v3, v5, v7, v5b, v1f, cols1)
-
-    for k in order:
+                coup = rb1[k // 2]
+                row0[:, bl(1 + k)] = coup.T.astype(BF16)
+                v1[bl(1 + k), :] = coup.astype(BF16)
+                v1f[bl(1 + k), :] = coup
+            yield k
+
+    onsite_two = []
+
+    def send_x2():
+        for k in (1, 0):
+            @pl.when(has[k])
+            def _():
+                coup2(k).start()
+        c0 = cols1[bl(0), :]
+        two = v1f[bl(0), :] + hubbard * (0.5 * (c0 + c0.T) - jnp.where(one_eye, 0.5, 0.0))
+        send2[...] = two
+        onsite_two.append(two)
+        for k in order:
+            @pl.when(has[k])
+            def _():
+                diag2(k).start()
+
+    density_columns(w, row0, v1, dk, sx, fb, v3, u, v1f, cols1, send_x2, arrived1)
+
+    for k in (3, 2):
         @pl.when(has[k])
         def _():
             coup2(k).start()
-    c0 = cols1[bl(0), :]
-    onsite_two = v1f[bl(0), :] + hubbard * (0.5 * (c0 + c0.T) - jnp.where(one_eye, 0.5, 0.0))
-    send2[...] = onsite_two
-    for k in order:
-        @pl.when(has[k])
-        def _():
-            diag2(k).start()
-    row0[:, bl(0)] = onsite_two.astype(BF16)
-    v1[bl(0), :] = onsite_two.astype(BF16)
-    v1f[bl(0), :] = onsite_two
+    two = onsite_two[0]
+    row0[:, bl(0)] = two.astype(BF16)
+    v1[bl(0), :] = two.astype(BF16)
+    v1f[bl(0), :] = two
     for k in range(4):
         v1f[bl(1 + k), :] = v1f[bl(1 + k), :] + 0.5 * hubbard * cols1[bl(1 + k), :]
-    for k in (0, 1, 2, 3):
-        @pl.when(has[k])
-        def _():
-            coup2(k ^ 1).wait_recv()
-            diag2(k ^ 1).wait_recv()
-    for k in range(4):
-        dk[k] = rd2[k].astype(BF16)
-        bk = v1f[bl(1 + k), :] + 0.5 * hubbard * rc2[k].T
-        v1f[bl(1 + k), :] = bk
-        v1[bl(1 + k), :] = bk.astype(BF16)
-        row0[:, bl(1 + k)] = bk.T.astype(BF16)
-
-    density_columns(w, row0, v1, dk, sx, fb, w13, v3, v5, v7, v5b, v1f, cols2)
-
-    for k in (2, 0):
-        @pl.when(has[k])
-        def _():
-            coup3(k).start()
+
+    def arrived2(slots):
+        for k in (2, 3, 1, 0):
+            @pl.when(has[k])
+            def _():
+                coup2(k ^ 1).wait_recv()
+                diag2(k ^ 1).wait_recv()
+            dk[k] = rd2[k].astype(BF16)
+            bk = v1f[bl(1 + k), :] + 0.5 * hubbard * rc2[k].T
+            v1f[bl(1 + k), :] = bk
+            v1[bl(1 + k), :] = bk.astype(BF16)
+            row0[:, bl(1 + k)] = bk.T.astype(BF16)
+            yield k
+
+    def send_x3():
+        @pl.when(has[0])
+        def _():
+            coup3(0).start()
+
+    density_columns(w, row0, v1, dk, sx, fb, v3, u, v1f, cols2, send_x3, arrived2)
+
+    @pl.when(has[2])
+    def _():
+        coup3(2).start()
     c0 = cols2[bl(0), :]
-    od_ref[0, 0] = 0.5 * (c0 + c0.T)
-    ox_ref[0, 0] = 0.5 * cols2[bl(2), :].T
-    oy_ref[0, 0] = 0.5 * cols2[bl(4), :].T
-    for k in (1, 3):
+    out_ref[0] = 0.5 * (c0 + c0.T)
+    half_x = 0.5 * cols2[bl(2), :].T
+    half_y = 0.5 * cols2[bl(4), :].T
+    for k in (3, 1):
         @pl.when(has[k])
         def _():
             coup3(k ^ 1).wait_recv()
-    ox_ref[0, 0] = ox_ref[0, 0] + 0.5 * rf3[0]
-    oy_ref[0, 0] = oy_ref[0, 0] + 0.5 * rf3[1]
+    out_ref[1] = half_x + 0.5 * rf3[0]
+    out_ref[2] = half_y + 0.5 * rf3[1]
     for k in range(4):
         @pl.when(has[k])
         def _():
@@ -250,6 +273,17 @@
             diag2(k).wait_send()
 
 
+def write_out(in_ref, od_ref, ox_ref, oy_ref, sems):
+    copies = [
+        pltpu.make_async_copy(in_ref.at[i], ref.at[0, 0], sems.at[i])
+        for i, ref in enumerate((od_ref, ox_ref, oy_ref))
+    ]
+    for copy in copies:
+        copy.start()
+    for copy in copies:
+        copy.wait()
+
+
 def per_device(diag_blocks, x_coupling, y_coupling, levels, listed):
     w = diag_blocks.shape[-1]
     n = 5 * w
@@ -257,11 +291,11 @@
     block = jax.ShapeDtypeStruct((1, 1, w, w), F32)
     any_spec = pl.BlockSpec(memory_space=pl.ANY)
     vmem_spec = pl.BlockSpec(memory_space=pltpu.VMEM)
-    return pl.pallas_call(
+    results = pl.pallas_call(
         functools.partial(kernel, sizes),
-        out_shape=(block, block, block),
+        out_shape=pltpu.VMEM((3, w, w), F32),
         in_specs=[any_spec] * 5,
-        out_specs=(vmem_spec,) * 3,
+        out_specs=vmem_spec,
         scratch_shapes=[
             pltpu.VMEM((w, w), F32),
             pltpu.VMEM((w, w), F32),
@@ -281,9 +315,6 @@
             pltpu.VMEM((4, w, w), BF16),
             pltpu.VMEM((n, n + w), BF16),
             pltpu.VMEM((n, n), BF16),
-            pltpu.VMEM((n, 2 * w), BF16),
-            pltpu.VMEM((n, w), F32),
-            pltpu.VMEM((n, w), F32),
             pltpu.VMEM((n, w), F32),
             pltpu.VMEM((n, w), BF16),
             pltpu.VMEM((n, w), F32),
@@ -293,6 +324,13 @@
         ],
         compiler_params=pltpu.CompilerParams(collective_id=0, has_side_effects=True),
     )(diag_blocks, x_coupling, y_coupling, levels, listed)
+    return pl.pallas_call(
+        write_out,
+        out_shape=(block, block, block),
+        in_specs=[vmem_spec],
+        out_specs=(any_spec,) * 3,
+        scratch_shapes=[pltpu.SemaphoreType.DMA((3,))],
+    )(results)
 
 
 def solution(mesh):

time: 25.8 us -> 24.8 us (0.961)
  local copies, waits for them, and re-layouts: 3 us -> 0.66 us
  Pallas kernels: 21.8 us -> 23.3 us
    unnamed x7 -> x2, local copies, waits for them, and re-layouts: 3 us -> 0.66 us
    pallas_call x1 -> x2, Pallas kernels: 21.8 us -> 23.3 us  [the longest x1 21.7 us: per_device(): pl.pallas_call(functools.partial(kernel, sizes), out_shape=pltpu.VMEM((3,...]
where the time goes in v2:
time: 24.8 us; the launch traced here: 24.6 us
  Pallas kernels  23.3 us (94%)
  local copies, waits for them, and re-layouts  0.66 us (3%)
  between operations  0.65 us (3%)
    pallas_call x1, Pallas kernels, per_device(): pl.pallas_call(functools.partial(kernel, sizes), out_shape=pltpu.VMEM((3,...  21.7 us
    pallas_call x1, Pallas kernels, per_device(): pl.pallas_call(write_out, out_shape=(block, block, block), in_specs=[vmem...  1.62 us
    unnamed x2, local copies, waits for them, and re-layouts  0.66 us

profile of v2, /device:TPU:0, one launch (start us, length us, event | category | flops | bytes accessed | tf_op | source)
XLA Modules:
  0.0 24.6 jit_solution(14371002422087786060)
XLA Ops:
  0.6 21.7 %shard_map.76.in_ref = f32[3,128,128]{2,1,0:T(8,128)S(1)} custom-call(f32[1,1,128,128]{3,2,1,0:T(8,128)} %diag_hbm.1, f32[1,1,128,128]{3,2,1,0:T(8,128)} %x_hbm.1, f32[1,1,128,128]{3,2,1,0:T(8,128)} %y_hbm.1, f32[1,1,128]{2,1,0:T(1,128)} %lev_hbm.1, s32[1,1,2]{2,1,0:T(1,128)} %list_hbm.1), custom_call_target="tpu_custom_call" | custom-call | tf_op jit(solution)/shard_map/pallas_call | solution.py:294
  22.3 0.0 copy-start
  22.3 0.7 %copy-done = f32[3,128,128]{2,1,0:T(8,128)} copy-done((f32[3,128,128]{2,1,0:T(8,128)}, f32[3,128,128]{2,1,0:T(8,128)S(1)}, u32[]{:S(2)}) %copy-start) | copy-done | bytes 196632
  23.0 1.6 %shard_map.77 = (f32[1,1,128,128]{3,2,1,0:T(8,128)}, f32[1,1,128,128]{3,2,1,0:T(8,128)}, f32[1,1,128,128]{3,2,1,0:T(8,128)}) custom-call(f32[3,128,128]{2,1,0:T(8,128)} %copy-done), custom_call_target="tpu_custom_call" | custom-call | tf_op jit(solution)/shard_map/pallas_call | solution.py:327
Async XLA Ops:
  22.3 0.7 %copy-start = (f32[3,128,128]{2,1,0:T(8,128)}, f32[3,128,128]{2,1,0:T(8,128)S(1)}, u32[]{:S(2)}) copy-start(f32[3,128,128]{2,1,0:T(8,128)S(1)} %shard_map.76.in_ref) | copy-start | bytes 589828

commit v3 on v2

--- a/solution.py
+++ b/solution.py
@@ -330,7 +330,7 @@
         in_specs=[vmem_spec],
         out_specs=(any_spec,) * 3,
         scratch_shapes=[pltpu.SemaphoreType.DMA((3,))],
-    )(results)
+    )(pltpu.with_memory_space_constraint(results, pltpu.VMEM))
 
 
 def solution(mesh):

time: 24.8 us -> 23.2 us (0.935)
  Pallas kernels: 23.3 us -> 22.4 us
  local copies, waits for them, and re-layouts: 0.66 us -> 0 us
    pallas_call x1, Pallas kernels: 1.62 us -> 0.7 us  [per_device(): pl.pallas_call(write_out, out_shape=(block, block, block), in_specs=[vmem...]
    unnamed x2 -> x0, local copies, waits for them, and re-layouts: 0.66 us -> none
where the time goes in v3:
time: 23.2 us; the launch traced here: 23 us
  Pallas kernels  22.4 us (97%)
  between operations  0.64 us (3%)
    pallas_call x1, Pallas kernels, per_device(): pl.pallas_call(functools.partial(kernel, sizes), out_shape=pltpu.VMEM((3,...  21.7 us
    pallas_call x1, Pallas kernels, per_device(): pl.pallas_call(write_out, out_shape=(block, block, block), in_specs=[vmem...  0.7 us

profile of v3, /device:TPU:0, one launch (start us, length us, event | category | flops | bytes accessed | tf_op | source)
XLA Modules:
  0.0 23.0 jit_solution(13855664688457139360)
XLA Ops:
  0.6 21.7 %shard_map.76.in_ref = f32[3,128,128]{2,1,0:T(8,128)S(1)} custom-call(f32[1,1,128,128]{3,2,1,0:T(8,128)} %diag_hbm.1, f32[1,1,128,128]{3,2,1,0:T(8,128)} %x_hbm.1, f32[1,1,128,128]{3,2,1,0:T(8,128)} %y_hbm.1, f32[1,1,128]{2,1,0:T(1,128)} %lev_hbm.1, s32[1,1,2]{2,1,0:T(1,128)} %list_hbm.1), custom_call_target="tpu_custom_call" | custom-call | tf_op jit(solution)/shard_map/pallas_call | solution.py:294
  22.3 0.7 %shard_map.77 = (f32[1,1,128,128]{3,2,1,0:T(8,128)}, f32[1,1,128,128]{3,2,1,0:T(8,128)}, f32[1,1,128,128]{3,2,1,0:T(8,128)}) custom-call(f32[3,128,128]{2,1,0:T(8,128)S(1)} %shard_map.76.in_ref), custom_call_target="tpu_custom_call" | custom-call | tf_op jit(solution)/shard_map/pallas_call | solution.py:327

commit v4 on v3

--- a/solution.py
+++ b/solution.py
@@ -185,19 +185,21 @@
         v1[bl(2 + 2 * axis), :] = coup_t.astype(BF16)
         v1f[bl(2 + 2 * axis), :] = coup_t
     def arrived1(slots):
-        for k in (2, 3, 1, 0):
-            @pl.when(has[k])
-            def _():
+        for group in ((2, 3), (1, 0)):
+            for k in group:
+                @pl.when(has[k])
+                def _():
+                    if k % 2 == 0:
+                        coup1(k ^ 1).wait_recv()
+                    diag1(k ^ 1).wait_recv()
+            for k in group:
+                dk[k] = rd1[k].astype(BF16)
                 if k % 2 == 0:
-                    coup1(k ^ 1).wait_recv()
-                diag1(k ^ 1).wait_recv()
-            dk[k] = rd1[k].astype(BF16)
-            if k % 2 == 0:
-                coup = rb1[k // 2]
-                row0[:, bl(1 + k)] = coup.T.astype(BF16)
-                v1[bl(1 + k), :] = coup.astype(BF16)
-                v1f[bl(1 + k), :] = coup
-            yield k
+                    coup = rb1[k // 2]
+                    row0[:, bl(1 + k)] = coup.T.astype(BF16)
+                    v1[bl(1 + k), :] = coup.astype(BF16)
+                    v1f[bl(1 + k), :] = coup
+            yield from group
 
     onsite_two = []
 
@@ -229,17 +231,19 @@
         v1f[bl(1 + k), :] = v1f[bl(1 + k), :] + 0.5 * hubbard * cols1[bl(1 + k), :]
 
     def arrived2(slots):
-        for k in (2, 3, 1, 0):
-            @pl.when(has[k])
-            def _():
-                coup2(k ^ 1).wait_recv()
-                diag2(k ^ 1).wait_recv()
-            dk[k] = rd2[k].astype(BF16)
-            bk = v1f[bl(1 + k), :] + 0.5 * hubbard * rc2[k].T
-            v1f[bl(1 + k), :] = bk
-            v1[bl(1 + k), :] = bk.astype(BF16)
-            row0[:, bl(1 + k)] = bk.T.astype(BF16)
-            yield k
+        for group in ((2, 3), (1, 0)):
+            for k in group:
+                @pl.when(has[k])
+                def _():
+                    coup2(k ^ 1).wait_recv()
+                    diag2(k ^ 1).wait_recv()
+            for k in group:
+                dk[k] = rd2[k].astype(BF16)
+                bk = v1f[bl(1 + k), :] + 0.5 * hubbard * rc2[k].T
+                v1f[bl(1 + k), :] = bk
+                v1[bl(1 + k), :] = bk.astype(BF16)
+                row0[:, bl(1 + k)] = bk.T.astype(BF16)
+            yield from group
 
     def send_x3():
         @pl.when(has[0])

time: 23.2 us -> 22.5 us (0.970)
  Pallas kernels: 22.4 us -> 21.7 us
    pallas_call x1, Pallas kernels: 21.7 us -> 21 us  [per_device(): pl.pallas_call(functools.partial(kernel, sizes), out_shape=pltpu.VMEM((3,...]
where the time goes in v4:
time: 22.5 us; the launch traced here: 22.3 us
  Pallas kernels  21.7 us (96%)
  between operations  0.64 us (3%)
    pallas_call x1, Pallas kernels, per_device(): pl.pallas_call(functools.partial(kernel, sizes), out_shape=pltpu.VMEM((3,...  21 us
    pallas_call x1, Pallas kernels, per_device(): pl.pallas_call(write_out, out_shape=(block, block, block), in_specs=[vmem...  0.7 us

profile of v4, /device:TPU:0, one launch (start us, length us, event | category | flops | bytes accessed | tf_op | source)
XLA Modules:
  0.0 22.3 jit_solution(12715608524295351402)
XLA Ops:
  0.6 21.0 %shard_map.76.in_ref = f32[3,128,128]{2,1,0:T(8,128)S(1)} custom-call(f32[1,1,128,128]{3,2,1,0:T(8,128)} %diag_hbm.1, f32[1,1,128,128]{3,2,1,0:T(8,128)} %x_hbm.1, f32[1,1,128,128]{3,2,1,0:T(8,128)} %y_hbm.1, f32[1,1,128]{2,1,0:T(1,128)} %lev_hbm.1, s32[1,1,2]{2,1,0:T(1,128)} %list_hbm.1), custom_call_target="tpu_custom_call" | custom-call | tf_op jit(solution)/shard_map/pallas_call | solution.py:298
  21.6 0.7 %shard_map.77 = (f32[1,1,128,128]{3,2,1,0:T(8,128)}, f32[1,1,128,128]{3,2,1,0:T(8,128)}, f32[1,1,128,128]{3,2,1,0:T(8,128)}) custom-call(f32[3,128,128]{2,1,0:T(8,128)S(1)} %shard_map.76.in_ref), custom_call_target="tpu_custom_call" | custom-call | tf_op jit(solution)/shard_map/pallas_call | solution.py:331

commit v5 on v4

--- a/solution.py
+++ b/solution.py
@@ -86,7 +86,7 @@
     sizes, diag_hbm, x_hbm, y_hbm, lev_hbm, list_hbm, out_ref,
     din, xin, yin, lin, fin, in_sems,
     send1, rd1, rb1, send2, rd2, rc2, rf3,
-    row0, v1, dk, sx, fb, v3, u, v1f, cols,
+    row0, v1, dk, sx, fb, v3, u, v1f, cols, rowf,
     send_sems, recv_sems,
 ):
     nx, ny = sizes
@@ -228,7 +228,7 @@
     v1[bl(0), :] = two.astype(BF16)
     v1f[bl(0), :] = two
     for k in range(4):
-        v1f[bl(1 + k), :] = v1f[bl(1 + k), :] + 0.5 * hubbard * cols1[bl(1 + k), :]
+        rowf[k] = (v1f[bl(1 + k), :] + 0.5 * hubbard * cols1[bl(1 + k), :]).T
 
     def arrived2(slots):
         for group in ((2, 3), (1, 0)):
@@ -239,10 +239,11 @@
                     diag2(k ^ 1).wait_recv()
             for k in group:
                 dk[k] = rd2[k].astype(BF16)
-                bk = v1f[bl(1 + k), :] + 0.5 * hubbard * rc2[k].T
+                btk = rowf[k] + 0.5 * hubbard * rc2[k]
+                row0[:, bl(1 + k)] = btk.astype(BF16)
+                bk = btk.T
                 v1f[bl(1 + k), :] = bk
                 v1[bl(1 + k), :] = bk.astype(BF16)
-                row0[:, bl(1 + k)] = bk.T.astype(BF16)
             yield from group
 
     def send_x3():
@@ -323,6 +324,7 @@
             pltpu.VMEM((n, w), BF16),
             pltpu.VMEM((n, w), F32),
             pltpu.VMEM((2, n, w), F32),
+            pltpu.VMEM((4, w, w), F32),
             pltpu.SemaphoreType.DMA((16,)),
             pltpu.SemaphoreType.DMA((16,)),
         ],

time: 22.5 us -> 22.4 us (level)
  no operation moved by 1% of the time
where the time goes in v5:
time: 22.4 us; the launch traced here: 22.2 us
  Pallas kernels  21.6 us (96%)
  between operations  0.64 us (3%)
    pallas_call x1, Pallas kernels, per_device(): pl.pallas_call(functools.partial(kernel, sizes), out_shape=pltpu.VMEM((3,...  20.9 us
    pallas_call x1, Pallas kernels, per_device(): pl.pallas_call(write_out, out_shape=(block, block, block), in_specs=[vmem...  0.7 us

profile of v5, /device:TPU:0, one launch (start us, length us, event | category | flops | bytes accessed | tf_op | source)
XLA Modules:
  0.0 22.2 jit_solution(10372890372090423799)
XLA Ops:
  0.6 20.9 %shard_map.76.in_ref = f32[3,128,128]{2,1,0:T(8,128)S(1)} custom-call(f32[1,1,128,128]{3,2,1,0:T(8,128)} %diag_hbm.1, f32[1,1,128,128]{3,2,1,0:T(8,128)} %x_hbm.1, f32[1,1,128,128]{3,2,1,0:T(8,128)} %y_hbm.1, f32[1,1,128]{2,1,0:T(1,128)} %lev_hbm.1, s32[1,1,2]{2,1,0:T(1,128)} %list_hbm.1), custom_call_target="tpu_custom_call" | custom-call | tf_op jit(solution)/shard_map/pallas_call | solution.py:299
  21.5 0.7 %shard_map.77 = (f32[1,1,128,128]{3,2,1,0:T(8,128)}, f32[1,1,128,128]{3,2,1,0:T(8,128)}, f32[1,1,128,128]{3,2,1,0:T(8,128)}) custom-call(f32[3,128,128]{2,1,0:T(8,128)S(1)} %shard_map.76.in_ref), custom_call_target="tpu_custom_call" | custom-call | tf_op jit(solution)/shard_map/pallas_call | solution.py:333
